TPU v7x, 32 devices: a whole 2x2x4 slice. The times are simulated.
32 devices in a mesh: row: 8 (over z, x), col: 4 (over y, core).
Axes of the slice: x: 2, y: 2, z: 4, core: 2. Of those that a mesh axis runs over, the one named last changes fastest.
Arguments:
- tokens: bfloat16 [2, 8192, 768], P(None, ('row', 'col')), may hold values from -6 to 6
- segments: int32 [2, 8192], P(None, ('row', 'col')), may hold values from 0 to 17, as said below
- positions: int32 [2, 8192], P(None, ('row', 'col')), may hold values from 0 to 799, as said below
- w_qkv: bfloat16 [768, 3, 768], P('row', None, 'col'), may hold values from -0.21875 to 0.21875
- w_out: bfloat16 [768, 768], P('col', 'row'), may hold values from -0.875 to 0.875
- w_gate_up: bfloat16 [768, 2, 3072], P('row', None, 'col'), may hold values from -0.21875 to 0.21875
- w_down: bfloat16 [3072, 768], P('col', 'row'), may hold values from -0.109375 to 0.109375
- norm_gain: bfloat16 [768, 2], P('row'), may hold values from 0.5 to 1.5
- norm_bias: bfloat16 [768, 2], P('row'), may hold values from -1.1953125 to 1.1953125
- cotangent: float32 [2, 8192, 768], P(None, ('row', 'col')), may hold values from -6 to 6
Outputs:
- layer_out: bfloat16 [2, 8192, 768], P(None, ('row', 'col'))
- input_grad: float32 [2, 8192, 768], P(None, ('row', 'col'))
- grad_qkv: float32 [768, 3, 768], P('row', None, 'col')
- grad_out: float32 [768, 768], P('col', 'row')
- grad_gate_up: float32 [768, 2, 3072], P('row', None, 'col')
- grad_down: float32 [3072, 768], P('col', 'row')
- grad_gain: float32 [768, 2], P('row')
- grad_bias: float32 [768, 2], P('row')
Inputs may be any that keep to these rules, and one draw needn't show every extreme that they name: `segments`: within each sequence documents are numbered from 0 upward and never fall; a document has at most 800 tokens and at least 60 unless it is the last of its sequence; some document has exactly 800 tokens, and in some sequence every document but the last has exactly 60 tokens. `positions`: the place of each token within its document, counted from 0.
All inputs are finite; a program needn't handle non-finite values.
Results may differ from a plain program's by a relative error of at most 0.017.
Values may be sent and summed in bfloat16 or wider, within the bound.
No kernel may reach another device: no remote copies, remote signals or barrier semaphores. Data moves between devices by JAX's collectives and lax.ppermute only.
A program may use at most 192 MiB of HBM per device.

v0:
```python
import math
import jax
import jax.numpy as jnp
from jax import lax
from jax.sharding import PartitionSpec as P

HD = 64
LEN = 1024
epsilon = 1e-12
rope_base = 1000.0
masked_score = -1e30


def in_blocks(array, dim, peers):
    dims = array.shape
    blocks = array.reshape(*dims[:dim], peers, dims[dim] // peers, *dims[dim + 1 :])
    return jnp.moveaxis(blocks, dim, 0)


def summed_on_arrival(array, axis, dim):
    blocks = in_blocks(array, dim, lax.axis_size(axis))
    arrived = lax.all_to_all(blocks, axis, split_axis=0, concat_axis=0, tiled=True)
    return arrived.astype(jnp.float32).sum(axis=0)


def sent_together(arrays, axis, dim, along):
    widths = [math.prod(a.shape[along:]) for a in arrays]
    both = jnp.concatenate(
        [a.reshape(*a.shape[:along], w) for a, w in zip(arrays, widths)], axis=along
    )
    out = summed_on_arrival(both, axis, dim)
    blocks = jnp.split(out, [sum(widths[:k]) for k in range(1, len(widths))], axis=along)
    return tuple((b.reshape(*out.shape[:along], *a.shape[along:]) for a, b in zip(arrays, blocks)))


def sent_together_2(arrays, axis, dim, along):
    widths = [a.shape[along] for a in arrays]
    both = jnp.concatenate(arrays, axis=along)
    out = summed_on_arrival(both, axis, dim)
    return tuple(jnp.split(out, [sum(widths[:k]) for k in range(1, len(widths))], axis=along))


def rope_tables(positions):
    half_dim = HD // 2
    freq = rope_base ** (-jnp.arange(half_dim, dtype=jnp.float32) / half_dim)
    angles = positions.astype(jnp.float32)[:, None] * freq[None, :]
    return (jnp.cos(angles), jnp.sin(angles))


def rotate(values, cosine, sine):
    half_dim = HD // 2
    first = values[..., :half_dim]
    second = values[..., half_dim:]
    cosine = cosine[:, None, :]
    sine = sine[:, None, :]
    return jnp.concatenate(
        [first * cosine - second * sine, second * cosine + first * sine], axis=-1
    )


def unrotate(grad_vals, cosine, sine):
    half_dim = HD // 2
    first = grad_vals[..., :half_dim]
    second = grad_vals[..., half_dim:]
    cosine = cosine[:, None, :]
    sine = sine[:, None, :]
    return jnp.concatenate(
        [first * cosine + second * sine, second * cosine - first * sine], axis=-1
    )


def normalize(hidden):
    centred = hidden - jnp.mean(hidden, axis=-1, keepdims=True)
    variance = jnp.mean(centred * centred, axis=-1, keepdims=True)
    inv_std = lax.rsqrt(variance + epsilon)
    return (centred * inv_std, inv_std)


def norm_back(grad_norm, normed, inv_std):
    return inv_std * (
        grad_norm
        - jnp.mean(grad_norm, axis=-1, keepdims=True)
        - normed * jnp.mean(grad_norm * normed, axis=-1, keepdims=True)
    )


def gather_tokens(values):
    return lax.all_gather(values, "col", axis=0, tiled=True)


def token_sums(left, right, contract):
    row_count = left.shape[0] // lax.axis_size("col")
    piece = lax.slice_in_dim(left, 0, lax.axis_size("col") * row_count, axis=0)
    return lax.psum_scatter(
        lax.dot_general(
            piece, right, (((1,), (contract,)), ((), ())), preferred_element_type=jnp.float32
        ).astype(jnp.bfloat16),
        "col",
        scatter_dimension=0,
        tiled=True,
    ).astype(jnp.float32)


def fetch_weights(w_qkv, w_out, w_gate_up, w_down, norm_gain, norm_bias):
    qkv_full, gate_up_full, gain_full, bias_full = (
        lax.all_gather(w_qkv, "row", axis=0, tiled=True),
        lax.all_gather(w_gate_up, "row", axis=0, tiled=True),
        lax.all_gather(norm_gain, "row", axis=0, tiled=True),
        lax.all_gather(norm_bias, "row", axis=0, tiled=True),
    )
    out_full, down_full = (
        lax.all_gather(w_out, "row", axis=1, tiled=True),
        lax.all_gather(w_down, "row", axis=1, tiled=True),
    )
    width = qkv_full.shape[0]
    return (
        qkv_full.reshape(width, -1),
        out_full,
        gate_up_full.reshape(width, -1),
        down_full,
        gain_full.astype(jnp.float32),
        bias_full.astype(jnp.float32),
    )


def key_window(seq_len, low_row):
    span = min(LEN, seq_len)
    return (low_row // span * span, span)


def attend(queries, keys, values, segment):
    seq_len = queries.shape[0]
    block_rows = min(512, LEN, seq_len)
    scale = 1.0 / math.sqrt(HD)
    outs_list = []
    totals_list = []
    for block_number in range(seq_len // block_rows):
        low_row = block_number * block_rows
        key_start, span = key_window(seq_len, low_row)
        rows_q = queries[low_row : low_row + block_rows]
        scores = (
            jnp.einsum("qhd,khd->hqk", rows_q, keys, preferred_element_type=jnp.float32) * scale
        )
        same_doc = (
            segment[low_row : low_row + block_rows, None]
            == segment[None, key_start : key_start + span]
        )
        scores = jnp.where(same_doc[None], scores, masked_score)
        row_max = jnp.max(scores, axis=-1, keepdims=True)
        expo = jnp.exp(scores - row_max)
        row_sum = jnp.sum(expo, axis=-1, keepdims=True)
        probs = (expo / row_sum).astype(jnp.bfloat16)
        outs_list.append(
            jnp.einsum("hqk,khd->qhd", probs, values, preferred_element_type=jnp.float32).astype(
                jnp.bfloat16
            )
        )
        totals_list.append(row_max + jnp.log(row_sum))
    return (jnp.concatenate(outs_list, axis=0), jnp.concatenate(totals_list, axis=1))


def attend_back(queries, keys, values, log_total, grad_att, segment):
    seq_len = queries.shape[0]
    block_rows = min(512, LEN, seq_len)
    scale = 1.0 / math.sqrt(HD)
    grad_q_list = []
    grad_k = jnp.zeros(keys.shape, jnp.float32)
    grad_v = jnp.zeros(values.shape, jnp.float32)
    for block_number in range(seq_len // block_rows):
        low_row = block_number * block_rows
        key_start, span = key_window(seq_len, low_row)
        rows_q = queries[low_row : low_row + block_rows]
        rows_grad = grad_att[low_row : low_row + block_rows]
        keys_seq = keys[key_start : key_start + span]
        values_seq = values[key_start : key_start + span]
        scores = (
            jnp.einsum("qhd,khd->hqk", rows_q, keys_seq, preferred_element_type=jnp.float32) * scale
        )
        same_doc = (
            segment[low_row : low_row + block_rows, None]
            == segment[None, key_start : key_start + span]
        )
        scores = jnp.where(same_doc[None], scores, masked_score)
        probs = jnp.exp(scores - log_total[:, low_row : low_row + block_rows])
        probs_low = probs.astype(jnp.bfloat16)
        grad_probs = jnp.einsum(
            "qhd,khd->hqk", rows_grad, values_seq, preferred_element_type=jnp.float32
        )
        delta_sum = jnp.sum(probs * grad_probs, axis=-1, keepdims=True)
        grad_scores = (probs * (grad_probs - delta_sum)).astype(jnp.bfloat16)
        grad_q_list.append(
            jnp.einsum("hqk,khd->qhd", grad_scores, keys_seq, preferred_element_type=jnp.float32)
            * scale
        )
        grad_k = grad_k.at[key_start : key_start + span].add(
            jnp.einsum("hqk,qhd->khd", grad_scores, rows_q, preferred_element_type=jnp.float32)
            * scale
        )
        grad_v = grad_v.at[key_start : key_start + span].add(
            jnp.einsum("hqk,qhd->khd", probs_low, rows_grad, preferred_element_type=jnp.float32)
        )
    return (jnp.concatenate(grad_q_list, axis=0), grad_k, grad_v)


def on_device(
    tokens, segments, positions, w_qkv, w_out, w_gate_up, w_down, norm_gain, norm_bias, cotangent
):
    doc_ids, doc_places = (
        lax.all_gather(segments, "col", axis=1, tiled=True),
        lax.all_gather(positions, "col", axis=1, tiled=True),
    )

    def current_weights():
        return fetch_weights(w_qkv, w_out, w_gate_up, w_down, norm_gain, norm_bias)

    def forward_step(carry, items):
        inputs, segment, place = items
        qkv_w, out_w, gate_up_w, down_w, gains, biases = current_weights()
        seq_inputs = gather_tokens(inputs)
        seq_len = seq_inputs.shape[0]
        proj = jnp.dot(seq_inputs, qkv_w, preferred_element_type=jnp.float32).reshape(
            seq_len, 3, -1, HD
        )
        cosine, sine = rope_tables(place)
        queries = rotate(proj[:, 0], cosine, sine).astype(jnp.bfloat16)
        keys = rotate(proj[:, 1], cosine, sine).astype(jnp.bfloat16)
        values = proj[:, 2].astype(jnp.bfloat16)
        attended, log_total = attend(queries, keys, values, segment)
        flat_attended = attended.reshape(seq_len, -1)
        branch = token_sums(flat_attended, out_w, 0)
        first_normed, first_inv = normalize(inputs.astype(jnp.float32) + branch)
        first_out = first_normed * gains[:, 0] + biases[:, 0]
        seq_normed = gather_tokens(first_out.astype(jnp.bfloat16))
        gate_up = jnp.dot(seq_normed, gate_up_w, preferred_element_type=jnp.float32)
        half_cols = gate_up.shape[1] // 2
        hidden = (jax.nn.silu(gate_up[:, :half_cols]) * gate_up[:, half_cols:]).astype(jnp.bfloat16)
        feed = token_sums(hidden, down_w, 0)
        second_normed, second_inv = normalize(first_out + feed)
        outputs = (second_normed * gains[:, 1] + biases[:, 1]).astype(jnp.bfloat16)
        kept = (
            seq_inputs,
            queries,
            keys,
            values,
            flat_attended,
            log_total,
            seq_normed,
            gate_up,
            first_normed,
            first_inv,
            second_normed,
            second_inv,
        )
        return (carry, (outputs, kept))

    unused, (layer_out, kept_all) = lax.scan(
        forward_step, jnp.zeros((), jnp.float32), (tokens, doc_ids, doc_places)
    )

    def backward_step(totals, items):
        grad_y, segment, place, kept = items
        (
            seq_inputs,
            queries,
            keys,
            values,
            flat_attended,
            log_total,
            seq_normed,
            gate_up,
            first_normed,
            first_inv,
            second_normed,
            second_inv,
        ) = kept
        total_qkv, total_out, total_gate_up, total_down, total_gain, total_bias = totals
        qkv_w, out_w, gate_up_w, down_w, gains, biases = current_weights()
        seq_len = seq_inputs.shape[0]
        gain_two = jnp.sum(grad_y * second_normed, axis=0)
        bias_two = jnp.sum(grad_y, axis=0)
        grad_h2 = norm_back(grad_y * gains[:, 1], second_normed, second_inv)
        seq_grad_feed = gather_tokens(grad_h2.astype(jnp.bfloat16))
        grad_hidden = lax.dot_general(
            seq_grad_feed, down_w, (((1,), (1,)), ((), ())), preferred_element_type=jnp.float32
        )
        half_cols = gate_up.shape[1] // 2
        gate = gate_up[:, :half_cols]
        up_part = gate_up[:, half_cols:]
        sigma = jax.nn.sigmoid(gate)
        silu_gate = gate * sigma
        grad_gate = grad_hidden * up_part * sigma * (1.0 + gate * (1.0 - sigma))
        grad_up = grad_hidden * silu_gate
        grad_gate_up = jnp.concatenate([grad_gate, grad_up], axis=1).astype(jnp.bfloat16)
        hidden = (silu_gate * up_part).astype(jnp.bfloat16)
        total_down = total_down + lax.dot_general(
            hidden, seq_grad_feed, (((0,), (0,)), ((), ())), preferred_element_type=jnp.float32
        )
        total_gate_up = total_gate_up + lax.dot_general(
            seq_normed, grad_gate_up, (((0,), (0,)), ((), ())), preferred_element_type=jnp.float32
        )
        grad_first = grad_h2 + token_sums(grad_gate_up, gate_up_w, 1)
        gain_one = jnp.sum(grad_first * first_normed, axis=0)
        bias_one = jnp.sum(grad_first, axis=0)
        grad_h1 = norm_back(grad_first * gains[:, 0], first_normed, first_inv)
        seq_grad_branch = gather_tokens(grad_h1.astype(jnp.bfloat16))
        total_out = total_out + lax.dot_general(
            flat_attended,
            seq_grad_branch,
            (((0,), (0,)), ((), ())),
            preferred_element_type=jnp.float32,
        )
        grad_att = lax.dot_general(
            seq_grad_branch, out_w, (((1,), (1,)), ((), ())), preferred_element_type=jnp.float32
        )
        grad_att = grad_att.astype(jnp.bfloat16).reshape(seq_len, -1, HD)
        grad_q, grad_k, grad_v = attend_back(queries, keys, values, log_total, grad_att, segment)
        cosine, sine = rope_tables(place)
        grad_proj = jnp.stack(
            [unrotate(grad_q, cosine, sine), unrotate(grad_k, cosine, sine), grad_v], axis=1
        )
        grad_proj = grad_proj.reshape(seq_len, -1).astype(jnp.bfloat16)
        total_qkv = total_qkv + lax.dot_general(
            seq_inputs, grad_proj, (((0,), (0,)), ((), ())), preferred_element_type=jnp.float32
        )
        grad_inputs = grad_h1 + token_sums(grad_proj, qkv_w, 1)
        total_gain = total_gain + jnp.stack([gain_one, gain_two], axis=1)
        total_bias = total_bias + jnp.stack([bias_one, bias_two], axis=1)
        return (
            (total_qkv, total_out, total_gate_up, total_down, total_gain, total_bias),
            grad_inputs,
        )

    width = tokens.shape[2]
    head_cols = w_qkv.shape[2]
    hidden_cols = w_gate_up.shape[2]
    zero_sums = (
        jnp.zeros((width, 3 * head_cols), jnp.float32),
        jnp.zeros((head_cols, width), jnp.float32),
        jnp.zeros((width, 2 * hidden_cols), jnp.float32),
        jnp.zeros((hidden_cols, width), jnp.float32),
        jnp.zeros((width, 2), jnp.float32),
        jnp.zeros((width, 2), jnp.float32),
    )
    totals, input_grad = lax.scan(
        backward_step, zero_sums, (cotangent, doc_ids, doc_places, kept_all)
    )
    total_qkv = totals[0].reshape(width, 3, head_cols)
    total_gate_up = totals[2].reshape(width, 2, hidden_cols)
    grad_qkv, grad_gate_up, grad_gain, grad_bias = sent_together(
        (
            total_qkv.astype(jnp.bfloat16),
            total_gate_up.astype(jnp.bfloat16),
            totals[4].astype(jnp.bfloat16),
            totals[5].astype(jnp.bfloat16),
        ),
        "row",
        0,
        1,
    )
    grad_out, grad_down = sent_together_2(
        (totals[1].astype(jnp.bfloat16), totals[3].astype(jnp.bfloat16)), "row", 1, 0
    )
    grad_gain, grad_bias = lax.psum((grad_gain, grad_bias), "col")
    return (
        layer_out,
        input_grad,
        grad_qkv,
        grad_out,
        grad_gate_up,
        grad_down,
        grad_gain,
        grad_bias,
    )


def solution(mesh):
    in_specs = (
        P(None, ("row", "col"), None),
        P(None, ("row", "col")),
        P(None, ("row", "col")),
        P("row", None, "col"),
        P("col", "row"),
        P("row", None, "col"),
        P("col", "row"),
        P("row", None),
        P("row", None),
        P(None, ("row", "col"), None),
    )
    out_specs = (
        P(None, ("row", "col"), None),
        P(None, ("row", "col"), None),
        P("row", None, "col"),
        P("col", "row"),
        P("row", None, "col"),
        P("col", "row"),
        P("row", None),
        P("row", None),
    )
    return jax.shard_map(
        on_device, mesh=mesh, in_specs=in_specs, out_specs=out_specs, check_vma=False
    )
```

profile of v0, /device:TPU:0, one launch (start us, length us, event | category | flops | bytes accessed | tf_op | source)
XLA Modules:
  0.0 1322.1 jit_solution(584793681520028164)
XLA Ops:
  7.3 6.4 all_gather.79
  13.8 6.9 all_gather.80
  25.1 542.4 %while.68 = (s32[]{:T(128)}, bf16[2,256,768]{2,1,0:T(8,128)(2,1)}, bf16[2,1024,768]{2,1,0:T(8,128)(2,1)}, bf16[2,1024,3,64]{1,3,2,0:T(8,128)(2,1)}, bf16[2,1024,...) while((s32[]{:T(128)}, bf16[2,256,768]{2,1,0:T(8,128)(2,1)}, ...), condition=%wide.region_11.12_spmd, body=%wide.region_0.11_spmd.sunk | while | flops 5697212928 | bytes 190405408 | solution.py:256
  26.1 37.9 %all_gather.99 = bf16[768,3,192]{2,1,0:T(4,128)(2,1)S(1)} all-gather(bf16[96,3,192]{2,1,0:T(4,128)(2,1)S(1)} %get-tuple-element.1742), channel_id=1, replica_groups=mesh['row'=8,'col'=4] {'row'}, dimensions={0}, use_global_device_ids=true | all-gather | bytes 995328 | tf_op jit(solution)/shard_map/while/body/eval_jaxpr/all_gather | solution.py:106
  66.8 31.1 %all_gather.100 = bf16[192,768]{0,1:T(8,128)(2,1)S(1)} all-gather(bf16[192,96]{0,1:T(8,128)(2,1)S(1)} %get-tuple-element.1745), channel_id=1, replica_groups=mesh['row'=8,'col'=4] {'row'}, dimensions={1}, use_global_device_ids=true | all-gather | bytes 331776 | tf_op jit(solution)/shard_map/while/body/eval_jaxpr/all_gather | solution.py:112
  115.7 18.5 %all-gather.11 = bf16[8,96,2]{1,2,0:T(2,128)(2,1)S(1)} all-gather(bf16[1,96,2]{1,2,0:T(2,128)(2,1)} %bitcast.350), channel_id=1, replica_groups=mesh['row'=8,'col'=4] {'row'}, dimensions={0}, use_global_device_ids=true | all-gather | bytes 3456 | tf_op jit(solution)/shard_map/while/body/eval_jaxpr/all_gather | solution.py:108
  134.3 16.4 %all-gather.10 = bf16[8,96,2]{1,2,0:T(2,128)(2,1)S(1)} all-gather(bf16[1,96,2]{1,2,0:T(2,128)(2,1)} %bitcast.349), channel_id=1, replica_groups=mesh['row'=8,'col'=4] {'row'}, dimensions={0}, use_global_device_ids=true | all-gather | bytes 3456 | tf_op jit(solution)/shard_map/while/body/eval_jaxpr/all_gather | solution.py:109
  157.1 38.9 %all-gather.28.cloned.1.call-done = bf16[768,2,768]{2,1,0:T(2,128)(2,1)} async-done(((bf16[96,2,768]{2,1,0:T(2,128)(2,1)}), bf16[768,2,768]{2,1,0:T(2,128)(2,1)}) %all-gather.28.cloned.1.call-update) | async-done | bytes 2359312 | tf_op jit(solution)/shard_map/while/body/eval_jaxpr/all_gather | solution.py:107
  198.1 18.2 %all-gather.26.cloned.1.call-done = bf16[1024,768]{1,0:T(8,128)(2,1)} async-done(((bf16[256,768]{1,0:T(8,128)(2,1)}), bf16[1024,768]{1,0:T(8,128)(2,1)}) %all-gather.26.cloned.1.call-update) | async-done | bytes 1572880 | tf_op jit(solution)/shard_map/while/body/eval_jaxpr/all_gather | solution.py:88
  216.3 7.5 bitcast_dynamic-update-slice_fusion.12
  223.8 35.6 %all-gather.22.cloned.1.call-done = bf16[768,768]{0,1:T(8,128)(2,1)} async-done(((bf16[768,96]{0,1:T(8,128)(2,1)}), bf16[768,768]{0,1:T(8,128)(2,1)}) %all-gather.22.cloned.1.call-update) | async-done | bytes 1179664 | tf_op jit(solution)/shard_map/while/body/eval_jaxpr/all_gather | solution.py:113
  259.5 6.2 convolution_convert_fusion.9
  276.4 16.5 %reduce-scatter.7.cloned.1.call-done = bf16[256,768]{1,0:T(8,128)(2,1)} async-done(((bf16[1024,768]{1,0:T(8,128)(2,1)}), bf16[256,768]{1,0:T(8,128)(2,1)}) %reduce-scatter.7.cloned.1.call-update) | async-done | bytes 393232 | tf_op jit(solution)/shard_map/while/body/eval_jaxpr/reduce_scatter | solution.py:94
  297.7 37.2 %all_gather.99 = bf16[768,3,192]{2,1,0:T(4,128)(2,1)S(1)} all-gather(bf16[96,3,192]{2,1,0:T(4,128)(2,1)S(1)} %get-tuple-element.1742), channel_id=1, replica_groups=mesh['row'=8,'col'=4] {'row'}, dimensions={0}, use_global_device_ids=true | all-gather | bytes 995328 | tf_op jit(solution)/shard_map/while/body/eval_jaxpr/all_gather | solution.py:106
  337.7 31.2 %all_gather.100 = bf16[192,768]{0,1:T(8,128)(2,1)S(1)} all-gather(bf16[192,96]{0,1:T(8,128)(2,1)S(1)} %get-tuple-element.1745), channel_id=1, replica_groups=mesh['row'=8,'col'=4] {'row'}, dimensions={1}, use_global_device_ids=true | all-gather | bytes 331776 | tf_op jit(solution)/shard_map/while/body/eval_jaxpr/all_gather | solution.py:112
  386.7 18.3 %all-gather.11 = bf16[8,96,2]{1,2,0:T(2,128)(2,1)S(1)} all-gather(bf16[1,96,2]{1,2,0:T(2,128)(2,1)} %bitcast.350), channel_id=1, replica_groups=mesh['row'=8,'col'=4] {'row'}, dimensions={0}, use_global_device_ids=true | all-gather | bytes 3456 | tf_op jit(solution)/shard_map/while/body/eval_jaxpr/all_gather | solution.py:108
  405.1 16.4 %all-gather.10 = bf16[8,96,2]{1,2,0:T(2,128)(2,1)S(1)} all-gather(bf16[1,96,2]{1,2,0:T(2,128)(2,1)} %bitcast.349), channel_id=1, replica_groups=mesh['row'=8,'col'=4] {'row'}, dimensions={0}, use_global_device_ids=true | all-gather | bytes 3456 | tf_op jit(solution)/shard_map/while/body/eval_jaxpr/all_gather | solution.py:109
  428.0 38.5 %all-gather.28.cloned.1.call-done = bf16[768,2,768]{2,1,0:T(2,128)(2,1)} async-done(((bf16[96,2,768]{2,1,0:T(2,128)(2,1)}), bf16[768,2,768]{2,1,0:T(2,128)(2,1)}) %all-gather.28.cloned.1.call-update) | async-done | bytes 2359312 | tf_op jit(solution)/shard_map/while/body/eval_jaxpr/all_gather | solution.py:107
  468.7 18.2 %all-gather.26.cloned.1.call-done = bf16[1024,768]{1,0:T(8,128)(2,1)} async-done(((bf16[256,768]{1,0:T(8,128)(2,1)}), bf16[1024,768]{1,0:T(8,128)(2,1)}) %all-gather.26.cloned.1.call-update) | async-done | bytes 1572880 | tf_op jit(solution)/shard_map/while/body/eval_jaxpr/all_gather | solution.py:88
  486.9 7.5 bitcast_dynamic-update-slice_fusion.12
  494.4 35.7 %all-gather.22.cloned.1.call-done = bf16[768,768]{0,1:T(8,128)(2,1)} async-done(((bf16[768,96]{0,1:T(8,128)(2,1)}), bf16[768,768]{0,1:T(8,128)(2,1)}) %all-gather.22.cloned.1.call-update) | async-done | bytes 1179664 | tf_op jit(solution)/shard_map/while/body/eval_jaxpr/all_gather | solution.py:113
  530.2 6.2 convolution_convert_fusion.9
  547.1 16.5 %reduce-scatter.7.cloned.1.call-done = bf16[256,768]{1,0:T(8,128)(2,1)} async-done(((bf16[1024,768]{1,0:T(8,128)(2,1)}), bf16[256,768]{1,0:T(8,128)(2,1)}) %reduce-scatter.7.cloned.1.call-update) | async-done | bytes 393232 | tf_op jit(solution)/shard_map/while/body/eval_jaxpr/reduce_scatter | solution.py:94
  568.7 603.9 %while.69 = (s32[]{:T(128)}, f32[768,576]{0,1:T(8,128)}, f32[192,768]{1,0:T(8,128)}, f32[768,1536]{1,0:T(8,128)}, f32[768,768]{1,0:T(8,128)}, /*index=5*/f32[768...) while((s32[]{:T(128)}, f32[768,576]{0,1:T(8,128)}, ...), condition=%wide.region_25.26_spmd.clone, body=%wide.region_12.25_spmd.clone.sunk | while | flops 11771122688 | bytes 393030208 | solution.py:344
  589.5 20.5 %all-gather.12 = bf16[8,96,2]{1,2,0:T(2,128)(2,1)S(1)} all-gather(bf16[1,96,2]{1,2,0:T(2,128)(2,1)} %bitcast.403), channel_id=1, replica_groups=mesh['row'=8,'col'=4] {'row'}, dimensions={0}, use_global_device_ids=true | all-gather | bytes 3456 | tf_op jit(solution)/shard_map/while/body/eval_jaxpr/all_gather | solution.py:108
  615.5 6.0 constant_dynamic-slice_fusion.22
  621.5 6.6 copy.127
  632.8 19.9 %all-gather.32.cloned.1.call-done = bf16[1024,768]{1,0:T(8,128)(2,1)} async-done(((bf16[256,768]{1,0:T(8,128)(2,1)}), bf16[1024,768]{1,0:T(8,128)(2,1)}) %all-gather.32.cloned.1.call-update) | async-done | bytes 1572880 | tf_op jit(solution)/shard_map/while/body/eval_jaxpr/all_gather | solution.py:88
  652.7 7.8 multiply_convert_fusion.13
  660.5 46.3 %all-gather.30.cloned.1.call-done = bf16[768,2,768]{2,1,0:T(2,128)(2,1)} async-done(((bf16[96,2,768]{2,1,0:T(2,128)(2,1)}), bf16[768,2,768]{2,1,0:T(2,128)(2,1)}) %all-gather.30.cloned.1.call-update) | async-done | bytes 2359312 | tf_op jit(solution)/shard_map/while/body/eval_jaxpr/all_gather | solution.py:107
  713.3 26.8 %reduce-scatter.9.cloned.1.call-done = bf16[256,768]{1,0:T(8,128)(2,1)} async-done(((bf16[1024,768]{1,0:T(8,128)(2,1)}), bf16[256,768]{1,0:T(8,128)(2,1)}) %reduce-scatter.9.cloned.1.call-update) | async-done | bytes 393232 | tf_op jit(solution)/shard_map/while/body/eval_jaxpr/reduce_scatter | solution.py:94
  744.3 37.3 %all_gather.108 = bf16[768,3,192]{2,1,0:T(4,128)(2,1)S(1)} all-gather(bf16[96,3,192]{2,1,0:T(4,128)(2,1)S(1)} %get-tuple-element.1842), channel_id=1, replica_groups=mesh['row'=8,'col'=4] {'row'}, dimensions={0}, use_global_device_ids=true | all-gather | bytes 995328 | tf_op jit(solution)/shard_map/while/body/eval_jaxpr/all_gather | solution.py:106
  784.5 31.0 %all_gather.107 = bf16[192,768]{0,1:T(8,128)(2,1)S(1)} all-gather(bf16[192,96]{0,1:T(8,128)(2,1)S(1)} %get-tuple-element.1837), channel_id=1, replica_groups=mesh['row'=8,'col'=4] {'row'}, dimensions={1}, use_global_device_ids=true | all-gather | bytes 331776 | tf_op jit(solution)/shard_map/while/body/eval_jaxpr/all_gather | solution.py:112
  852.9 7.5 select_add_fusion.7
  868.2 9.8 reduce-scatter.11.cloned.1.call-done
  880.8 20.6 %all-gather.12 = bf16[8,96,2]{1,2,0:T(2,128)(2,1)S(1)} all-gather(bf16[1,96,2]{1,2,0:T(2,128)(2,1)} %bitcast.403), channel_id=1, replica_groups=mesh['row'=8,'col'=4] {'row'}, dimensions={0}, use_global_device_ids=true | all-gather | bytes 3456 | tf_op jit(solution)/shard_map/while/body/eval_jaxpr/all_gather | solution.py:108
  913.0 6.6 copy.127
  924.1 19.9 %all-gather.32.cloned.1.call-done = bf16[1024,768]{1,0:T(8,128)(2,1)} async-done(((bf16[256,768]{1,0:T(8,128)(2,1)}), bf16[1024,768]{1,0:T(8,128)(2,1)}) %all-gather.32.cloned.1.call-update) | async-done | bytes 1572880 | tf_op jit(solution)/shard_map/while/body/eval_jaxpr/all_gather | solution.py:88
  944.0 7.8 multiply_convert_fusion.13
  951.8 46.5 %all-gather.30.cloned.1.call-done = bf16[768,2,768]{2,1,0:T(2,128)(2,1)} async-done(((bf16[96,2,768]{2,1,0:T(2,128)(2,1)}), bf16[768,2,768]{2,1,0:T(2,128)(2,1)}) %all-gather.30.cloned.1.call-update) | async-done | bytes 2359312 | tf_op jit(solution)/shard_map/while/body/eval_jaxpr/all_gather | solution.py:107
  1004.8 26.8 %reduce-scatter.9.cloned.1.call-done = bf16[256,768]{1,0:T(8,128)(2,1)} async-done(((bf16[1024,768]{1,0:T(8,128)(2,1)}), bf16[256,768]{1,0:T(8,128)(2,1)}) %reduce-scatter.9.cloned.1.call-update) | async-done | bytes 393232 | tf_op jit(solution)/shard_map/while/body/eval_jaxpr/reduce_scatter | solution.py:94
  1035.7 37.0 %all_gather.108 = bf16[768,3,192]{2,1,0:T(4,128)(2,1)S(1)} all-gather(bf16[96,3,192]{2,1,0:T(4,128)(2,1)S(1)} %get-tuple-element.1842), channel_id=1, replica_groups=mesh['row'=8,'col'=4] {'row'}, dimensions={0}, use_global_device_ids=true | all-gather | bytes 995328 | tf_op jit(solution)/shard_map/while/body/eval_jaxpr/all_gather | solution.py:106
  1075.6 31.2 %all_gather.107 = bf16[192,768]{0,1:T(8,128)(2,1)S(1)} all-gather(bf16[192,96]{0,1:T(8,128)(2,1)S(1)} %get-tuple-element.1837), channel_id=1, replica_groups=mesh['row'=8,'col'=4] {'row'}, dimensions={1}, use_global_device_ids=true | all-gather | bytes 331776 | tf_op jit(solution)/shard_map/while/body/eval_jaxpr/all_gather | solution.py:112
  1144.2 8.9 select_add_fusion.7
  1162.6 8.0 reduce-scatter.11.cloned.1.call-done
  1194.5 25.8 %all-to-all-done.1 = bf16[8,960,96]{1,2,0:T(8,128)(2,1)} async-done(((bf16[8,960,96]{1,2,0:T(8,128)(2,1)}), bf16[8,960,96]{1,2,0:T(8,128)(2,1)}, u32[]{:S(2)}, u32[]{:S(2)}) %all-to-all-start.1) | async-done | bytes 1474592 | tf_op jit(solution)/shard_map/all_to_all | solution.py:22
  1227.4 71.7 %all-to-all-done = bf16[8,96,2116]{2,1,0:T(8,128)(2,1)S(1)} async-done(((bf16[8,96,2116]{2,1,0:T(8,128)(2,1)}), bf16[8,96,2116]{2,1,0:T(8,128)(2,1)S(1)}, u32[]{:S(2)}, u32[]{:S(2)}) %all-to-all-start) | async-done | bytes 3250208 | tf_op jit(solution)/shard_map/all_to_all | solution.py:22
  1299.9 11.5 all-reduce
  (595 shorter events, 276.9 us)
Async XLA Ops:
  25.1 73.9 %copy-start.9 = (bf16[96,3,192]{2,1,0:T(4,128)(2,1)}, bf16[96,3,192]{2,1,0:T(4,128)(2,1)S(1)}, u32[]{:S(2)}) copy-start(bf16[96,3,192]{2,1,0:T(4,128)(2,1)S(1)} %get-tuple-element.1742) | copy-start | bytes 331780 | tf_op jit(solution)/shard_map/while
  25.1 73.9 %copy-start.25 = (bf16[192,96]{0,1:T(8,128)(2,1)}, bf16[192,96]{0,1:T(8,128)(2,1)S(1)}, u32[]{:S(2)}) copy-start(bf16[192,96]{0,1:T(8,128)(2,1)S(1)} %get-tuple-element.1745) | copy-start | bytes 110596 | tf_op jit(solution)/shard_map/while
  25.1 74.0 %all-gather.24.cloned.1.call-start = ((), (), s32[]{:S(2)}) async-start(), calls=%async_computation.7 | async-start | bytes 1966080 | tf_op jit(solution)/shard_map/while/body/eval_jaxpr/all_gather | solution.py:88
  26.0 125.4 %reduce-scatter.5.cloned.1.call-start = ((), (), s32[]{:S(2)}) async-start(), calls=%async_computation.8 | async-start | bytes 1966080 | tf_op jit(solution)/shard_map/while/body/eval_jaxpr/reduce_scatter | solution.py:94
  114.9 81.1 %all-gather.28.cloned.1.call-start = ((), (), s32[]{:S(2)}) async-start(), calls=%async_computation.10 | async-start | bytes 2654208 | tf_op jit(solution)/shard_map/while/body/eval_jaxpr/all_gather | solution.py:107
  115.6 100.7 %all-gather.26.cloned.1.call-start = ((), (), s32[]{:S(2)}) async-start(), calls=%async_computation.9 | async-start | bytes 1966080 | tf_op jit(solution)/shard_map/while/body/eval_jaxpr/all_gather | solution.py:88
  156.4 103.0 %all-gather.22.cloned.1.call-start = ((), (), s32[]{:S(2)}) async-start(), calls=%async_computation.6 | async-start | bytes 1327104 | tf_op jit(solution)/shard_map/while/body/eval_jaxpr/all_gather | solution.py:113
  157.0 135.8 %reduce-scatter.7.cloned.1.call-start = ((), (), s32[]{:S(2)}) async-start(), calls=%async_computation.11 | async-start | bytes 1966080 | tf_op jit(solution)/shard_map/while/body/eval_jaxpr/reduce_scatter | solution.py:94
  271.9 21.0 %copy-start.42 = (f32[256]{0:T(256)S(1)}, f32[256]{0:T(256)}, u32[]{:S(2)}) copy-start(f32[256]{0:T(256)} %copy-done.40) | copy-start | bytes 3076 | tf_op jit(solution)/shard_map/while
  271.9 21.0 %copy-start.45 = (f32[256]{0:T(256)S(1)}, f32[256]{0:T(256)}, u32[]{:S(2)}) copy-start(f32[256]{0:T(256)} %copy-done.43) | copy-start | bytes 3076 | tf_op jit(solution)/shard_map/while
  275.1 20.6 %copy-start.57 = (f32[2,256,1]{1,2,0:T(1,128)S(1)}, f32[2,256,1]{1,2,0:T(1,128)}, u32[]{:S(2)}) copy-start(f32[2,256,1]{1,2,0:T(1,128)} %get-tuple-element.1714) | copy-start | bytes 6148 | tf_op jit(solution)/shard_map/while
  275.1 20.6 %copy-start.46 = (f32[768]{0:T(1024)S(1)}, f32[768]{0:T(1024)}, u32[]{:S(2)}) copy-start(f32[768]{0:T(1024)} %get-tuple-element.1602) | copy-start | bytes 9220 | tf_op jit(solution)/shard_map/while
  275.1 20.6 %copy-start.47 = (f32[768]{0:T(1024)S(1)}, f32[768]{0:T(1024)}, u32[]{:S(2)}) copy-start(f32[768]{0:T(1024)} %get-tuple-element.1603) | copy-start | bytes 9220 | tf_op jit(solution)/shard_map/while
  296.8 73.3 %copy-start.9 = (bf16[96,3,192]{2,1,0:T(4,128)(2,1)}, bf16[96,3,192]{2,1,0:T(4,128)(2,1)S(1)}, u32[]{:S(2)}) copy-start(bf16[96,3,192]{2,1,0:T(4,128)(2,1)S(1)} %get-tuple-element.1742) | copy-start | bytes 331780 | tf_op jit(solution)/shard_map/while
  296.8 73.3 %copy-start.25 = (bf16[192,96]{0,1:T(8,128)(2,1)}, bf16[192,96]{0,1:T(8,128)(2,1)S(1)}, u32[]{:S(2)}) copy-start(bf16[192,96]{0,1:T(8,128)(2,1)S(1)} %get-tuple-element.1745) | copy-start | bytes 110596 | tf_op jit(solution)/shard_map/while
  296.8 73.4 %all-gather.24.cloned.1.call-start = ((), (), s32[]{:S(2)}) async-start(), calls=%async_computation.7 | async-start | bytes 1966080 | tf_op jit(solution)/shard_map/while/body/eval_jaxpr/all_gather | solution.py:88
  297.7 124.6 %reduce-scatter.5.cloned.1.call-start = ((), (), s32[]{:S(2)}) async-start(), calls=%async_computation.8 | async-start | bytes 1966080 | tf_op jit(solution)/shard_map/while/body/eval_jaxpr/reduce_scatter | solution.py:94
  386.0 80.6 %all-gather.28.cloned.1.call-start = ((), (), s32[]{:S(2)}) async-start(), calls=%async_computation.10 | async-start | bytes 2654208 | tf_op jit(solution)/shard_map/while/body/eval_jaxpr/all_gather | solution.py:107
  386.7 100.2 %all-gather.26.cloned.1.call-start = ((), (), s32[]{:S(2)}) async-start(), calls=%async_computation.9 | async-start | bytes 1966080 | tf_op jit(solution)/shard_map/while/body/eval_jaxpr/all_gather | solution.py:88
  427.3 102.9 %all-gather.22.cloned.1.call-start = ((), (), s32[]{:S(2)}) async-start(), calls=%async_computation.6 | async-start | bytes 1327104 | tf_op jit(solution)/shard_map/while/body/eval_jaxpr/all_gather | solution.py:113
  428.0 135.6 %reduce-scatter.7.cloned.1.call-start = ((), (), s32[]{:S(2)}) async-start(), calls=%async_computation.11 | async-start | bytes 1966080 | tf_op jit(solution)/shard_map/while/body/eval_jaxpr/reduce_scatter | solution.py:94
  542.6 21.0 %copy-start.42 = (f32[256]{0:T(256)S(1)}, f32[256]{0:T(256)}, u32[]{:S(2)}) copy-start(f32[256]{0:T(256)} %copy-done.40) | copy-start | bytes 3076 | tf_op jit(solution)/shard_map/while
  542.6 21.0 %copy-start.45 = (f32[256]{0:T(256)S(1)}, f32[256]{0:T(256)}, u32[]{:S(2)}) copy-start(f32[256]{0:T(256)} %copy-done.43) | copy-start | bytes 3076 | tf_op jit(solution)/shard_map/while
  545.8 20.6 %copy-start.57 = (f32[2,256,1]{1,2,0:T(1,128)S(1)}, f32[2,256,1]{1,2,0:T(1,128)}, u32[]{:S(2)}) copy-start(f32[2,256,1]{1,2,0:T(1,128)} %get-tuple-element.1714) | copy-start | bytes 6148 | tf_op jit(solution)/shard_map/while
  545.8 20.6 %copy-start.46 = (f32[768]{0:T(1024)S(1)}, f32[768]{0:T(1024)}, u32[]{:S(2)}) copy-start(f32[768]{0:T(1024)} %get-tuple-element.1602) | copy-start | bytes 9220 | tf_op jit(solution)/shard_map/while
  545.8 20.6 %copy-start.47 = (f32[768]{0:T(1024)S(1)}, f32[768]{0:T(1024)}, u32[]{:S(2)}) copy-start(f32[768]{0:T(1024)} %get-tuple-element.1603) | copy-start | bytes 9220 | tf_op jit(solution)/shard_map/while
  588.7 155.6 %copy-start.11 = (bf16[96,3,192]{2,1,0:T(4,128)(2,1)}, bf16[96,3,192]{2,1,0:T(4,128)(2,1)S(1)}, u32[]{:S(2)}) copy-start(bf16[96,3,192]{2,1,0:T(4,128)(2,1)S(1)} %get-tuple-element.1842) | copy-start | bytes 331780 | tf_op jit(solution)/shard_map/while
  588.7 195.8 %copy-start.27 = (bf16[192,96]{0,1:T(8,128)(2,1)}, bf16[192,96]{0,1:T(8,128)(2,1)S(1)}, u32[]{:S(2)}) copy-start(bf16[192,96]{0,1:T(8,128)(2,1)S(1)} %get-tuple-element.1837) | copy-start | bytes 110596 | tf_op jit(solution)/shard_map/while
  588.7 44.1 %all-gather.34.cloned.1.call-start = ((), (), s32[]{:S(2)}) async-start(), calls=%async_computation.14 | async-start | bytes 1327104 | tf_op jit(solution)/shard_map/while/body/eval_jaxpr/all_gather | solution.py:113
  589.4 63.2 %all-gather.32.cloned.1.call-start = ((), (), s32[]{:S(2)}) async-start(), calls=%async_computation.13 | async-start | bytes 1966080 | tf_op jit(solution)/shard_map/while/body/eval_jaxpr/all_gather | solution.py:88
  614.8 92.0 %all-gather.30.cloned.1.call-start = ((), (), s32[]{:S(2)}) async-start(), calls=%async_computation.12 | async-start | bytes 2654208 | tf_op jit(solution)/shard_map/while/body/eval_jaxpr/all_gather | solution.py:107
  615.4 124.7 %reduce-scatter.9.cloned.1.call-start = ((), (), s32[]{:S(2)}) async-start(), calls=%async_computation.15 | async-start | bytes 1966080 | tf_op jit(solution)/shard_map/while/body/eval_jaxpr/reduce_scatter | solution.py:94
  713.2 112.7 %all-gather.36.cloned.1.call-start = ((), (), s32[]{:S(2)}) async-start(), calls=%async_computation.16 | async-start | bytes 1966080 | tf_op jit(solution)/shard_map/while/body/eval_jaxpr/all_gather | solution.py:88
  741.7 42.8 %copy-start.56 = (f32[2,3,1024,1]{2,1,3,0:T(4,128)S(1)}, f32[2,3,1024,1]{2,1,3,0:T(4,128)}, u32[]{:S(2)}) copy-start(f32[2,3,1024,1]{2,1,3,0:T(4,128)} %get-tuple-element.1827) | copy-start | bytes 73732 | tf_op jit(solution)/shard_map/while
  744.2 71.9 %copy-start.6 = (bf16[2,1024,3,64]{1,3,2,0:T(8,128)(2,1)S(1)}, bf16[2,1024,3,64]{1,3,2,0:T(8,128)(2,1)}, u32[]{:S(2)}) copy-start(bf16[2,1024,3,64]{1,3,2,0:T(8,128)(2,1)} %get-tuple-element.1824) | copy-start | bytes 2359300 | tf_op jit(solution)/shard_map/while
  744.2 133.8 %reduce-scatter.11.cloned.1.call-start = ((), (), s32[]{:S(2)}) async-start(), calls=%async_computation.17 | async-start | bytes 1966080 | tf_op jit(solution)/shard_map/while/body/eval_jaxpr/reduce_scatter | solution.py:94
  880.0 155.7 %copy-start.11 = (bf16[96,3,192]{2,1,0:T(4,128)(2,1)}, bf16[96,3,192]{2,1,0:T(4,128)(2,1)S(1)}, u32[]{:S(2)}) copy-start(bf16[96,3,192]{2,1,0:T(4,128)(2,1)S(1)} %get-tuple-element.1842) | copy-start | bytes 331780 | tf_op jit(solution)/shard_map/while
  880.0 195.6 %copy-start.27 = (bf16[192,96]{0,1:T(8,128)(2,1)}, bf16[192,96]{0,1:T(8,128)(2,1)S(1)}, u32[]{:S(2)}) copy-start(bf16[192,96]{0,1:T(8,128)(2,1)S(1)} %get-tuple-element.1837) | copy-start | bytes 110596 | tf_op jit(solution)/shard_map/while
  880.0 44.1 %all-gather.34.cloned.1.call-start = ((), (), s32[]{:S(2)}) async-start(), calls=%async_computation.14 | async-start | bytes 1327104 | tf_op jit(solution)/shard_map/while/body/eval_jaxpr/all_gather | solution.py:113
  880.7 63.3 %all-gather.32.cloned.1.call-start = ((), (), s32[]{:S(2)}) async-start(), calls=%async_computation.13 | async-start | bytes 1966080 | tf_op jit(solution)/shard_map/while/body/eval_jaxpr/all_gather | solution.py:88
  906.1 92.1 %all-gather.30.cloned.1.call-start = ((), (), s32[]{:S(2)}) async-start(), calls=%async_computation.12 | async-start | bytes 2654208 | tf_op jit(solution)/shard_map/while/body/eval_jaxpr/all_gather | solution.py:107
  906.9 124.7 %reduce-scatter.9.cloned.1.call-start = ((), (), s32[]{:S(2)}) async-start(), calls=%async_computation.15 | async-start | bytes 1966080 | tf_op jit(solution)/shard_map/while/body/eval_jaxpr/reduce_scatter | solution.py:94
  1004.7 112.6 %all-gather.36.cloned.1.call-start = ((), (), s32[]{:S(2)}) async-start(), calls=%async_computation.16 | async-start | bytes 1966080 | tf_op jit(solution)/shard_map/while/body/eval_jaxpr/all_gather | solution.py:88
  1033.1 42.4 %copy-start.56 = (f32[2,3,1024,1]{2,1,3,0:T(4,128)S(1)}, f32[2,3,1024,1]{2,1,3,0:T(4,128)}, u32[]{:S(2)}) copy-start(f32[2,3,1024,1]{2,1,3,0:T(4,128)} %get-tuple-element.1827) | copy-start | bytes 73732 | tf_op jit(solution)/shard_map/while
  1035.6 71.8 %copy-start.6 = (bf16[2,1024,3,64]{1,3,2,0:T(8,128)(2,1)S(1)}, bf16[2,1024,3,64]{1,3,2,0:T(8,128)(2,1)}, u32[]{:S(2)}) copy-start(bf16[2,1024,3,64]{1,3,2,0:T(8,128)(2,1)} %get-tuple-element.1824) | copy-start | bytes 2359300 | tf_op jit(solution)/shard_map/while
  1035.6 134.9 %reduce-scatter.11.cloned.1.call-start = ((), (), s32[]{:S(2)}) async-start(), calls=%async_computation.17 | async-start | bytes 1966080 | tf_op jit(solution)/shard_map/while/body/eval_jaxpr/reduce_scatter | solution.py:94
  1177.7 42.6 %all-to-all-start.1 = ((bf16[8,960,96]{1,2,0:T(8,128)(2,1)}), bf16[8,960,96]{1,2,0:T(8,128)(2,1)}, u32[]{:S(2)}, u32[]{:S(2)}) async-start(bf16[8,960,96]{1,2,0:T(8,128)(2,1)} %bitcast.41), calls=%async_computation.5 | async-start | bytes 3145728 | tf_op jit(solution)/shard_map/all_to_all | solution.py:22
  1220.3 78.7 %all-to-all-start = ((bf16[8,96,2116]{2,1,0:T(8,128)(2,1)}), bf16[8,96,2116]{2,1,0:T(8,128)(2,1)S(1)}, u32[]{:S(2)}, u32[]{:S(2)}) async-start(bf16[8,96,2116]{2,1,0:T(8,128)(2,1)} %concatenate.100), calls=%async_computation.4 | async-start | bytes 6684672 | tf_op jit(solution)/shard_map/all_to_all | solution.py:22
  (123 other events, 633.4 us)
Sparse Core Ops, SparseCore 0:
  27.5 20.1 all-gather.23
  115.0 26.4 reduce-scatter.4
  143.9 52.0 all-gather.27
  198.1 18.1 all-gather.25
  218.3 41.0 all-gather.21
  265.9 26.9 reduce-scatter.6
  299.2 19.6 all-gather.23
  386.1 25.9 reduce-scatter.4
  414.5 52.0 all-gather.27
  468.6 18.1 all-gather.25
  489.1 41.0 all-gather.21
  536.6 26.9 reduce-scatter.6
  591.7 41.0 all-gather.33
  634.2 18.4 all-gather.31
  654.7 52.0 all-gather.29
  713.4 26.7 reduce-scatter.8
  744.3 19.6 all-gather.35
  851.6 26.3 reduce-scatter.10
  883.0 41.0 all-gather.33
  925.5 18.4 all-gather.31
  946.2 52.0 all-gather.29
  1004.8 26.6 reduce-scatter.8
  1035.7 19.6 all-gather.35
  1142.9 27.5 reduce-scatter.10
where the time goes:
time: 1340 us; the launch traced here: 1320 us
  waiting for transfers between devices  535 us (40%)
  blocking collectives  409 us (31%)
  matrix products  162 us (12%)
  local copies, waits for them, and re-layouts  95.7 us (7%)
  other arithmetic  73 us (5%)
  loops' own time  22.6 us (2%)
  between operations  14.7 us (1%)
    all_gather x4, waiting for transfers between devices, fetch_weights(): lax.all_gather(w_gate_up, 'row', axis=0, tiled=True)  170 us
    all_gather x4, blocking collectives, fetch_weights(): lax.all_gather(w_qkv, 'row', axis=0, tiled=True)  149 us
    all_gather x4, blocking collectives, fetch_weights(): lax.all_gather(w_out, 'row', axis=1, tiled=True)  124 us
    reduce_scatter x8, waiting for transfers between devices, token_sums(): lax.psum_scatter(lax.dot_general(piece, right, (((1,), (contract,)), ((),...  104 us
    all_to_all x2, waiting for transfers between devices, summed_on_arrival(): lax.all_to_all(blocks, axis, split_axis=0, concat_axis=0, tiled=True)  97.5 us
    all_gather x4, waiting for transfers between devices, fetch_weights(): lax.all_gather(w_down, 'row', axis=1, tiled=True)  80.7 us
    all_gather x4, blocking collectives, fetch_weights(): lax.all_gather(norm_gain, 'row', axis=0, tiled=True)  77.9 us
    all_gather x8, waiting for transfers between devices, gather_tokens(): return lax.all_gather(values, 'col', axis=0, tiled=True)  76.2 us
  transfers between devices with their start and end apart: 26, of which 20 were waited for; matrix products, arithmetic and copies ran while one was open for 14% of the time, Pallas kernels for 0%

commit v1 on v0

--- a/solution.py
+++ b/solution.py
@@ -9,6 +9,22 @@
 epsilon = 1e-12
 rope_base = 1000.0
 masked_score = -1e30
+
+
+def bands_end(m, axis_key):
+    v1 = lax.axis_size(axis_key)
+    r_now = lax.axis_index(axis_key)
+    current_value, carry_out = (v1, r_now)
+    p_next, now = (m, 1)
+    while now < current_value:
+        k_now = lax.ppermute(
+            p_next, axis_key, [(hop_no, hop_no ^ now) for hop_no in range(current_value)]
+        )
+        next_value = jnp.concatenate([p_next, k_now], 0)
+        response = jnp.concatenate([k_now, p_next], 0)
+        p_next = jnp.where(carry_out & now == 0, next_value, response)
+        now = 2 * now
+    return p_next
 
 
 def in_blocks(array, dim, peers):
@@ -85,7 +101,7 @@
 
 
 def gather_tokens(values):
-    return lax.all_gather(values, "col", axis=0, tiled=True)
+    return bands_end(values, "col")
 
 
 def token_sums(left, right, contract):

time: 1340 us -> 1240 us (0.925)
  waiting for transfers between devices: 535 us -> 399 us
  other arithmetic: 73 us -> 93.4 us
    all_gather x8 -> x0, waiting for transfers between devices: 76.2 us -> none  [gather_tokens(): return lax.all_gather(values, 'col', axis=0, tiled=True)]
    reduce_scatter x8, waiting for transfers between devices: 104 us -> 38.2 us  [token_sums(): lax.psum_scatter(lax.dot_general(piece, right, (((1,), (contract,)), ((),...]
    ppermute x0 -> x16, waiting for transfers between devices: none -> 38.6 us  [bands_end(): lax.ppermute(p_next, axis_key, [(hop_no, hop_no ^ now) for hop_no in rang...]
    all_gather x4, waiting for transfers between devices: 80.7 us -> 64.3 us  [fetch_weights(): lax.all_gather(w_down, 'row', axis=1, tiled=True)]
    all_gather x4, waiting for transfers between devices: 170 us -> 156 us  [fetch_weights(): lax.all_gather(w_gate_up, 'row', axis=0, tiled=True)]
  transfers between devices with their start and end apart: 26 -> 34, of which waited for: 20 -> 20; matrix products, arithmetic and copies ran while one was open for 14% -> 16% of each run, Pallas kernels for 0% -> 0%
where the time goes in v1:
time: 1240 us; the launch traced here: 1220 us
  blocking collectives  414 us (33%)
  waiting for transfers between devices  399 us (32%)
  matrix products  170 us (14%)
  other arithmetic  93.4 us (8%)
  local copies, waits for them, and re-layouts  87.5 us (7%)
  loops' own time  26.9 us (2%)
  starting transfers between devices  19.3 us (2%)
  between operations  14.2 us (1%)
    all_gather x4, waiting for transfers between devices, fetch_weights(): lax.all_gather(w_gate_up, 'row', axis=0, tiled=True)  156 us
    all_gather x4, blocking collectives, fetch_weights(): lax.all_gather(w_qkv, 'row', axis=0, tiled=True)  149 us
    all_gather x4, blocking collectives, fetch_weights(): lax.all_gather(w_out, 'row', axis=1, tiled=True)  129 us
    all_to_all x2, waiting for transfers between devices, summed_on_arrival(): lax.all_to_all(blocks, axis, split_axis=0, concat_axis=0, tiled=True)  97.5 us
    all_gather x4, blocking collectives, fetch_weights(): lax.all_gather(norm_gain, 'row', axis=0, tiled=True)  78.2 us
    all_gather x4, waiting for transfers between devices, fetch_weights(): lax.all_gather(w_down, 'row', axis=1, tiled=True)  64.3 us
    ppermute x16, waiting for transfers between devices, bands_end(): lax.ppermute(p_next, axis_key, [(hop_no, hop_no ^ now) for hop_no in rang...  38.6 us
    reduce_scatter x8, waiting for transfers between devices, token_sums(): lax.psum_scatter(lax.dot_general(piece, right, (((1,), (contract,)), ((),...  38.2 us
  transfers between devices with their start and end apart: 34, of which 20 were waited for; matrix products, arithmetic and copies ran while one was open for 16% of the time, Pallas kernels for 0%

profile of v1, /device:TPU:0, one launch (start us, length us, event | category | flops | bytes accessed | tf_op | source)
XLA Modules:
  0.0 1224.1 jit_solution(17027895789283126235)
XLA Ops:
  7.3 6.4 all_gather.59
  13.8 6.9 all_gather.60
  26.5 508.4 %while.68 = (s32[]{:T(128)}, bf16[2,256,768]{2,1,0:T(8,128)(2,1)}, bf16[2,1024,768]{2,1,0:T(8,128)(2,1)}, bf16[2,1024,3,64]{1,3,2,0:T(8,128)(2,1)}, bf16[2,1024,...) while((s32[]{:T(128)}, bf16[2,256,768]{2,1,0:T(8,128)(2,1)}, ...), condition=%wide.region_11.12_spmd, body=%wide.region_0.11_spmd.sunk | while | flops 5732602368 | bytes 167994992 | solution.py:272
  27.5 37.9 %all_gather.75 = bf16[768,3,192]{2,1,0:T(4,128)(2,1)S(1)} all-gather(bf16[96,3,192]{2,1,0:T(4,128)(2,1)} %get-tuple-element.1746), channel_id=1, replica_groups=mesh['row'=8,'col'=4] {'row'}, dimensions={0}, use_global_device_ids=true | all-gather | bytes 995328 | tf_op jit(solution)/shard_map/while/body/eval_jaxpr/all_gather | solution.py:122
  71.2 31.2 %all_gather.76 = bf16[192,768]{0,1:T(8,128)(2,1)S(1)} all-gather(bf16[192,96]{0,1:T(8,128)(2,1)} %get-tuple-element.1749), channel_id=1, replica_groups=mesh['row'=8,'col'=4] {'row'}, dimensions={1}, use_global_device_ids=true | all-gather | bytes 331776 | tf_op jit(solution)/shard_map/while/body/eval_jaxpr/all_gather | solution.py:128
  122.0 18.6 %all-gather.8 = bf16[8,96,2]{1,2,0:T(2,128)(2,1)S(1)} all-gather(bf16[1,96,2]{1,2,0:T(2,128)(2,1)S(1)} %bitcast.456), channel_id=1, replica_groups=mesh['row'=8,'col'=4] {'row'}, dimensions={0}, use_global_device_ids=true | all-gather | bytes 3456 | tf_op jit(solution)/shard_map/while/body/eval_jaxpr/all_gather | solution.py:124
  140.7 16.2 %all-gather.7 = bf16[8,96,2]{1,2,0:T(2,128)(2,1)S(1)} all-gather(bf16[1,96,2]{1,2,0:T(2,128)(2,1)S(1)} %bitcast.458), channel_id=1, replica_groups=mesh['row'=8,'col'=4] {'row'}, dimensions={0}, use_global_device_ids=true | all-gather | bytes 3456 | tf_op jit(solution)/shard_map/while/body/eval_jaxpr/all_gather | solution.py:125
  164.8 37.2 %all-gather.17.cloned.1.call-done = bf16[768,2,768]{2,1,0:T(2,128)(2,1)} async-done(((bf16[96,2,768]{2,1,0:T(2,128)(2,1)}), bf16[768,2,768]{2,1,0:T(2,128)(2,1)}) %all-gather.17.cloned.1.call-update) | async-done | bytes 2359312 | tf_op jit(solution)/shard_map/while/body/eval_jaxpr/all_gather | solution.py:123
  204.1 7.6 bitcast_dynamic-update-slice_fusion.10
  211.7 32.1 %all-gather.15.cloned.1.call-done = bf16[768,768]{0,1:T(8,128)(2,1)} async-done(((bf16[768,96]{0,1:T(8,128)(2,1)}), bf16[768,768]{0,1:T(8,128)(2,1)}) %all-gather.15.cloned.1.call-update) | async-done | bytes 1179664 | tf_op jit(solution)/shard_map/while/body/eval_jaxpr/all_gather | solution.py:129
  243.8 6.2 convolution_convert_fusion.9
  263.2 14.0 %reduce-scatter.7.cloned.1.call-done = bf16[256,768]{1,0:T(8,128)(2,1)} async-done(((bf16[1024,768]{1,0:T(8,128)(2,1)}), bf16[256,768]{1,0:T(8,128)(2,1)}) %reduce-scatter.7.cloned.1.call-update) | async-done | bytes 393232 | tf_op jit(solution)/shard_map/while/body/eval_jaxpr/reduce_scatter | solution.py:110
  281.7 37.8 %all_gather.75 = bf16[768,3,192]{2,1,0:T(4,128)(2,1)S(1)} all-gather(bf16[96,3,192]{2,1,0:T(4,128)(2,1)} %get-tuple-element.1746), channel_id=1, replica_groups=mesh['row'=8,'col'=4] {'row'}, dimensions={0}, use_global_device_ids=true | all-gather | bytes 995328 | tf_op jit(solution)/shard_map/while/body/eval_jaxpr/all_gather | solution.py:122
  325.0 31.4 %all_gather.76 = bf16[192,768]{0,1:T(8,128)(2,1)S(1)} all-gather(bf16[192,96]{0,1:T(8,128)(2,1)} %get-tuple-element.1749), channel_id=1, replica_groups=mesh['row'=8,'col'=4] {'row'}, dimensions={1}, use_global_device_ids=true | all-gather | bytes 331776 | tf_op jit(solution)/shard_map/while/body/eval_jaxpr/all_gather | solution.py:128
  375.9 18.5 %all-gather.8 = bf16[8,96,2]{1,2,0:T(2,128)(2,1)S(1)} all-gather(bf16[1,96,2]{1,2,0:T(2,128)(2,1)S(1)} %bitcast.456), channel_id=1, replica_groups=mesh['row'=8,'col'=4] {'row'}, dimensions={0}, use_global_device_ids=true | all-gather | bytes 3456 | tf_op jit(solution)/shard_map/while/body/eval_jaxpr/all_gather | solution.py:124
  394.5 16.2 %all-gather.7 = bf16[8,96,2]{1,2,0:T(2,128)(2,1)S(1)} all-gather(bf16[1,96,2]{1,2,0:T(2,128)(2,1)S(1)} %bitcast.458), channel_id=1, replica_groups=mesh['row'=8,'col'=4] {'row'}, dimensions={0}, use_global_device_ids=true | all-gather | bytes 3456 | tf_op jit(solution)/shard_map/while/body/eval_jaxpr/all_gather | solution.py:125
  418.8 37.2 %all-gather.17.cloned.1.call-done = bf16[768,2,768]{2,1,0:T(2,128)(2,1)} async-done(((bf16[96,2,768]{2,1,0:T(2,128)(2,1)}), bf16[768,2,768]{2,1,0:T(2,128)(2,1)}) %all-gather.17.cloned.1.call-update) | async-done | bytes 2359312 | tf_op jit(solution)/shard_map/while/body/eval_jaxpr/all_gather | solution.py:123
  458.1 7.5 bitcast_dynamic-update-slice_fusion.10
  465.6 32.2 %all-gather.15.cloned.1.call-done = bf16[768,768]{0,1:T(8,128)(2,1)} async-done(((bf16[768,96]{0,1:T(8,128)(2,1)}), bf16[768,768]{0,1:T(8,128)(2,1)}) %all-gather.15.cloned.1.call-update) | async-done | bytes 1179664 | tf_op jit(solution)/shard_map/while/body/eval_jaxpr/all_gather | solution.py:129
  497.8 6.2 convolution_convert_fusion.9
  517.2 13.9 %reduce-scatter.7.cloned.1.call-done = bf16[256,768]{1,0:T(8,128)(2,1)} async-done(((bf16[1024,768]{1,0:T(8,128)(2,1)}), bf16[256,768]{1,0:T(8,128)(2,1)}) %reduce-scatter.7.cloned.1.call-update) | async-done | bytes 393232 | tf_op jit(solution)/shard_map/while/body/eval_jaxpr/reduce_scatter | solution.py:110
  536.1 539.1 %while.69 = (s32[]{:T(128)}, f32[768,576]{0,1:T(8,128)}, f32[192,768]{1,0:T(8,128)}, f32[768,1536]{1,0:T(8,128)}, f32[768,768]{1,0:T(8,128)}, /*index=5*/f32[768...) while((s32[]{:T(128)}, f32[768,576]{0,1:T(8,128)}, ...), condition=%wide.region_25.26_spmd.clone, body=%wide.region_12.25_spmd.clone.sunk | while | flops 11806512128 | bytes 363707328 | solution.py:360
  558.4 20.5 %all-gather.9 = bf16[8,96,2]{1,2,0:T(2,128)(2,1)S(1)} all-gather(bf16[1,96,2]{1,2,0:T(2,128)(2,1)} %bitcast.457), channel_id=1, replica_groups=mesh['row'=8,'col'=4] {'row'}, dimensions={0}, use_global_device_ids=true | all-gather | bytes 3456 | tf_op jit(solution)/shard_map/while/body/eval_jaxpr/all_gather | solution.py:124
  586.2 5.9 constant_dynamic-slice_fusion.19
  592.1 6.6 copy.127
  598.7 6.7 collective-permute-done.5
  605.3 7.9 multiply_convert_fusion.13
  613.2 40.6 %all-gather.19.cloned.1.call-done = bf16[768,2,768]{2,1,0:T(2,128)(2,1)} async-done(((bf16[96,2,768]{2,1,0:T(2,128)(2,1)}), bf16[768,2,768]{2,1,0:T(2,128)(2,1)}) %all-gather.19.cloned.1.call-update) | async-done | bytes 2359312 | tf_op jit(solution)/shard_map/while/body/eval_jaxpr/all_gather | solution.py:123
  661.0 33.2 %all_gather.77 = bf16[192,768]{0,1:T(8,128)(2,1)} all-gather(bf16[192,96]{0,1:T(8,128)(2,1)S(1)} %copy-done.14), channel_id=1, replica_groups=mesh['row'=8,'col'=4] {'row'}, dimensions={1}, use_global_device_ids=true | all-gather | bytes 331776 | tf_op jit(solution)/shard_map/while/body/eval_jaxpr/all_gather | solution.py:128
  703.9 37.0 %all_gather.80 = bf16[768,3,192]{2,1,0:T(4,128)(2,1)S(1)} all-gather(bf16[96,3,192]{2,1,0:T(4,128)(2,1)} %get-tuple-element.1852), channel_id=1, replica_groups=mesh['row'=8,'col'=4] {'row'}, dimensions={0}, use_global_device_ids=true | all-gather | bytes 995328 | tf_op jit(solution)/shard_map/while/body/eval_jaxpr/all_gather | solution.py:122
  750.0 9.4 collective-permute-done.7
  784.6 7.1 select_add_fusion.8
  791.8 7.2 select_add_fusion.7
  805.3 6.6 reduce-scatter.11.cloned.1.call-done
  815.5 20.6 %all-gather.9 = bf16[8,96,2]{1,2,0:T(2,128)(2,1)S(1)} all-gather(bf16[1,96,2]{1,2,0:T(2,128)(2,1)} %bitcast.457), channel_id=1, replica_groups=mesh['row'=8,'col'=4] {'row'}, dimensions={0}, use_global_device_ids=true | all-gather | bytes 3456 | tf_op jit(solution)/shard_map/while/body/eval_jaxpr/all_gather | solution.py:124
  849.3 6.6 copy.127
  855.9 6.7 collective-permute-done.5
  862.6 7.9 multiply_convert_fusion.13
  870.5 40.6 %all-gather.19.cloned.1.call-done = bf16[768,2,768]{2,1,0:T(2,128)(2,1)} async-done(((bf16[96,2,768]{2,1,0:T(2,128)(2,1)}), bf16[768,2,768]{2,1,0:T(2,128)(2,1)}) %all-gather.19.cloned.1.call-update) | async-done | bytes 2359312 | tf_op jit(solution)/shard_map/while/body/eval_jaxpr/all_gather | solution.py:123
  918.3 33.2 %all_gather.77 = bf16[192,768]{0,1:T(8,128)(2,1)} all-gather(bf16[192,96]{0,1:T(8,128)(2,1)S(1)} %copy-done.14), channel_id=1, replica_groups=mesh['row'=8,'col'=4] {'row'}, dimensions={1}, use_global_device_ids=true | all-gather | bytes 331776 | tf_op jit(solution)/shard_map/while/body/eval_jaxpr/all_gather | solution.py:128
  961.2 36.6 %all_gather.80 = bf16[768,3,192]{2,1,0:T(4,128)(2,1)S(1)} all-gather(bf16[96,3,192]{2,1,0:T(4,128)(2,1)} %get-tuple-element.1852), channel_id=1, replica_groups=mesh['row'=8,'col'=4] {'row'}, dimensions={0}, use_global_device_ids=true | all-gather | bytes 995328 | tf_op jit(solution)/shard_map/while/body/eval_jaxpr/all_gather | solution.py:122
  1007.7 9.0 collective-permute-done.7
  1041.9 8.0 select_add_fusion.8
  1049.9 7.9 select_add_fusion.7
  1091.2 5.9 concatenate.260
  1097.1 25.8 %all-to-all-done.1 = bf16[8,960,96]{1,2,0:T(8,128)(2,1)} async-done(((bf16[8,960,96]{1,2,0:T(8,128)(2,1)}), bf16[8,960,96]{1,2,0:T(8,128)(2,1)}, u32[]{:S(2)}, u32[]{:S(2)}) %all-to-all-start.1) | async-done | bytes 1474592 | tf_op jit(solution)/shard_map/all_to_all | solution.py:38
  1129.9 71.7 %all-to-all-done = bf16[8,96,2116]{2,1,0:T(8,128)(2,1)S(1)} async-done(((bf16[8,96,2116]{2,1,0:T(8,128)(2,1)}), bf16[8,96,2116]{2,1,0:T(8,128)(2,1)S(1)}, u32[]{:S(2)}, u32[]{:S(2)}) %all-to-all-start) | async-done | bytes 3250208 | tf_op jit(solution)/shard_map/all_to_all | solution.py:38
  1202.4 11.5 all-reduce
  (583 shorter events, 287.1 us)
Async XLA Ops:
  26.5 131.2 %reduce-scatter.5.cloned.1.call-start = ((), (), s32[]{:S(2)}) async-start(), calls=%async_computation.8 | async-start | bytes 1966080 | tf_op jit(solution)/shard_map/while/body/eval_jaxpr/reduce_scatter | solution.py:110
  26.5 38.9 %collective-permute-start = (bf16[256,768]{1,0:T(8,128)(2,1)S(1)}, bf16[256,768]{1,0:T(8,128)(2,1)}, u32[]{:S(2)}, u32[]{:S(2)}) collective-permute-start(bf16[256,768]{1,0:T(8,128)(2,1)S(1)} %dynamic-slice_bitcast_fusion.14), channel_id=1, source_target_pairs={{0,1},{1,0},{2,3},{3,2},{4,5},{5,4},{6,7},{7,6},{8,9},{9,8},{10,11... | collective-permute-start | bytes 1179656 | tf_op jit(solution)/shard_map/while/body/eval_jaxpr/ppermute | solution.py:20
  67.6 36.6 %collective-permute-start.1 = (bf16[512,768]{1,0:T(8,128)(2,1)}, bf16[512,768]{1,0:T(8,128)(2,1)}, u32[]{:S(2)}, u32[]{:S(2)}) collective-permute-start(bf16[512,768]{1,0:T(8,128)(2,1)} %maximum_select_fusion.22), channel_id=1, source_target_pairs={{0,2},{1,3},{2,0},{3,1},{4,6},{5,7},{6,4},{7,5},{8,10},{9,11},{10,... | collective-permute-start | bytes 2359304 | tf_op jit(solution)/shard_map/while/body/eval_jaxpr/ppermute | solution.py:20
  118.6 22.1 %copy-start.52 = (bf16[96,2]{0,1:T(2,128)(2,1)S(1)}, bf16[96,2]{0,1:T(2,128)(2,1)}, u32[]{:S(2)}) copy-start(bf16[96,2]{0,1:T(2,128)(2,1)} %get-tuple-element.1751) | copy-start | bytes 1156 | tf_op jit(solution)/shard_map/while
  120.5 81.5 %all-gather.17.cloned.1.call-start = ((), (), s32[]{:S(2)}) async-start(), calls=%async_computation.7 | async-start | bytes 2654208 | tf_op jit(solution)/shard_map/while/body/eval_jaxpr/all_gather | solution.py:123
  121.2 122.6 %all-gather.15.cloned.1.call-start = ((), (), s32[]{:S(2)}) async-start(), calls=%async_computation.6 | async-start | bytes 1327104 | tf_op jit(solution)/shard_map/while/body/eval_jaxpr/all_gather | solution.py:129
  122.0 155.1 %reduce-scatter.7.cloned.1.call-start = ((), (), s32[]{:S(2)}) async-start(), calls=%async_computation.9 | async-start | bytes 1966080 | tf_op jit(solution)/shard_map/while/body/eval_jaxpr/reduce_scatter | solution.py:110
  161.3 1.8 collective-permute-start.2
  163.4 40.6 %collective-permute-start.3 = (bf16[512,768]{1,0:T(8,128)(2,1)S(1)}, bf16[512,768]{1,0:T(8,128)(2,1)}, u32[]{:S(2)}, u32[]{:S(2)}) collective-permute-start(bf16[512,768]{1,0:T(8,128)(2,1)S(1)} %maximum_select_fusion.23), channel_id=1, source_target_pairs={{0,2},{1,3},{2,0},{3,1},{4,6},{5,7},{6,4},{7,5},{8,10},{9,11},{10,... | collective-permute-start | bytes 2359304 | tf_op jit(solution)/shard_map/while/body/eval_jaxpr/ppermute | solution.py:20
  257.0 20.2 %copy-start.29 = (f32[256]{0:T(256)S(1)}, f32[256]{0:T(256)}, u32[]{:S(2)}) copy-start(f32[256]{0:T(256)} %copy-done.27) | copy-start | bytes 3076 | tf_op jit(solution)/shard_map/while
  257.0 20.2 %copy-start.32 = (f32[256]{0:T(256)S(1)}, f32[256]{0:T(256)}, u32[]{:S(2)}) copy-start(f32[256]{0:T(256)} %copy-done.30) | copy-start | bytes 3076 | tf_op jit(solution)/shard_map/while
  260.0 19.7 %copy-start.53 = (f32[2,256,1]{1,2,0:T(1,128)S(1)}, f32[2,256,1]{1,2,0:T(1,128)}, u32[]{:S(2)}) copy-start(f32[2,256,1]{1,2,0:T(1,128)} %get-tuple-element.1716) | copy-start | bytes 6148 | tf_op jit(solution)/shard_map/while
  260.0 19.8 %copy-start.38 = (f32[768]{0:T(1024)S(1)}, f32[768]{0:T(1024)}, u32[]{:S(2)}) copy-start(f32[768]{0:T(1024)} %get-tuple-element.1602) | copy-start | bytes 9220 | tf_op jit(solution)/shard_map/while
  260.0 19.8 %copy-start.39 = (f32[768]{0:T(1024)S(1)}, f32[768]{0:T(1024)}, u32[]{:S(2)}) copy-start(f32[768]{0:T(1024)} %get-tuple-element.1603) | copy-start | bytes 9220 | tf_op jit(solution)/shard_map/while
  280.9 130.5 %reduce-scatter.5.cloned.1.call-start = ((), (), s32[]{:S(2)}) async-start(), calls=%async_computation.8 | async-start | bytes 1966080 | tf_op jit(solution)/shard_map/while/body/eval_jaxpr/reduce_scatter | solution.py:110
  280.9 38.5 %collective-permute-start = (bf16[256,768]{1,0:T(8,128)(2,1)S(1)}, bf16[256,768]{1,0:T(8,128)(2,1)}, u32[]{:S(2)}, u32[]{:S(2)}) collective-permute-start(bf16[256,768]{1,0:T(8,128)(2,1)S(1)} %dynamic-slice_bitcast_fusion.14), channel_id=1, source_target_pairs={{0,1},{1,0},{2,3},{3,2},{4,5},{5,4},{6,7},{7,6},{8,9},{9,8},{10,11... | collective-permute-start | bytes 1179656 | tf_op jit(solution)/shard_map/while/body/eval_jaxpr/ppermute | solution.py:20
  321.7 36.6 %collective-permute-start.1 = (bf16[512,768]{1,0:T(8,128)(2,1)}, bf16[512,768]{1,0:T(8,128)(2,1)}, u32[]{:S(2)}, u32[]{:S(2)}) collective-permute-start(bf16[512,768]{1,0:T(8,128)(2,1)} %maximum_select_fusion.22), channel_id=1, source_target_pairs={{0,2},{1,3},{2,0},{3,1},{4,6},{5,7},{6,4},{7,5},{8,10},{9,11},{10,... | collective-permute-start | bytes 2359304 | tf_op jit(solution)/shard_map/while/body/eval_jaxpr/ppermute | solution.py:20
  372.6 21.8 %copy-start.52 = (bf16[96,2]{0,1:T(2,128)(2,1)S(1)}, bf16[96,2]{0,1:T(2,128)(2,1)}, u32[]{:S(2)}) copy-start(bf16[96,2]{0,1:T(2,128)(2,1)} %get-tuple-element.1751) | copy-start | bytes 1156 | tf_op jit(solution)/shard_map/while
  374.5 81.5 %all-gather.17.cloned.1.call-start = ((), (), s32[]{:S(2)}) async-start(), calls=%async_computation.7 | async-start | bytes 2654208 | tf_op jit(solution)/shard_map/while/body/eval_jaxpr/all_gather | solution.py:123
  375.1 122.7 %all-gather.15.cloned.1.call-start = ((), (), s32[]{:S(2)}) async-start(), calls=%async_computation.6 | async-start | bytes 1327104 | tf_op jit(solution)/shard_map/while/body/eval_jaxpr/all_gather | solution.py:129
  375.8 155.3 %reduce-scatter.7.cloned.1.call-start = ((), (), s32[]{:S(2)}) async-start(), calls=%async_computation.9 | async-start | bytes 1966080 | tf_op jit(solution)/shard_map/while/body/eval_jaxpr/reduce_scatter | solution.py:110
  415.1 1.8 collective-permute-start.2
  417.2 40.9 %collective-permute-start.3 = (bf16[512,768]{1,0:T(8,128)(2,1)S(1)}, bf16[512,768]{1,0:T(8,128)(2,1)}, u32[]{:S(2)}, u32[]{:S(2)}) collective-permute-start(bf16[512,768]{1,0:T(8,128)(2,1)S(1)} %maximum_select_fusion.23), channel_id=1, source_target_pairs={{0,2},{1,3},{2,0},{3,1},{4,6},{5,7},{6,4},{7,5},{8,10},{9,11},{10,... | collective-permute-start | bytes 2359304 | tf_op jit(solution)/shard_map/while/body/eval_jaxpr/ppermute | solution.py:20
  510.9 20.2 %copy-start.29 = (f32[256]{0:T(256)S(1)}, f32[256]{0:T(256)}, u32[]{:S(2)}) copy-start(f32[256]{0:T(256)} %copy-done.27) | copy-start | bytes 3076 | tf_op jit(solution)/shard_map/while
  510.9 20.2 %copy-start.32 = (f32[256]{0:T(256)S(1)}, f32[256]{0:T(256)}, u32[]{:S(2)}) copy-start(f32[256]{0:T(256)} %copy-done.30) | copy-start | bytes 3076 | tf_op jit(solution)/shard_map/while
  514.1 19.7 %copy-start.39 = (f32[768]{0:T(1024)S(1)}, f32[768]{0:T(1024)}, u32[]{:S(2)}) copy-start(f32[768]{0:T(1024)} %get-tuple-element.1603) | copy-start | bytes 9220 | tf_op jit(solution)/shard_map/while
  557.0 103.5 %copy-start.17 = (s32[2,1024]{1,0:T(2,128)}, s32[2,1024]{1,0:T(2,128)S(1)}, u32[]{:S(2)}) copy-start(s32[2,1024]{1,0:T(2,128)S(1)} %get-tuple-element.1835) | copy-start | bytes 24580 | tf_op jit(solution)/shard_map/while
  557.0 48.3 %all-gather.21.cloned.1.call-start = ((), (), s32[]{:S(2)}) async-start(), calls=%async_computation.11 | async-start | bytes 1327104 | tf_op jit(solution)/shard_map/while/body/eval_jaxpr/all_gather | solution.py:129
  557.7 96.2 %all-gather.19.cloned.1.call-start = ((), (), s32[]{:S(2)}) async-start(), calls=%async_computation.10 | async-start | bytes 2654208 | tf_op jit(solution)/shard_map/while/body/eval_jaxpr/all_gather | solution.py:123
  558.3 141.8 %reduce-scatter.9.cloned.1.call-start = ((), (), s32[]{:S(2)}) async-start(), calls=%async_computation.12 | async-start | bytes 1966080 | tf_op jit(solution)/shard_map/while/body/eval_jaxpr/reduce_scatter | solution.py:110
  583.5 1.8 collective-permute-start.4
  585.6 19.8 %copy-start.8 = (bf16[512,768]{1,0:T(8,128)(2,1)}, bf16[512,768]{1,0:T(8,128)(2,1)S(1)}, u32[]{:S(2)}) copy-start(bf16[512,768]{1,0:T(8,128)(2,1)S(1)} %maximum_select_fusion.27) | copy-start | bytes 2359300 | tf_op jit(solution)/shard_map/while
  585.6 19.8 %collective-permute-start.5 = (bf16[512,768]{1,0:T(8,128)(2,1)S(1)}, bf16[512,768]{1,0:T(8,128)(2,1)}, u32[]{:S(2)}, u32[]{:S(2)}) collective-permute-start(bf16[512,768]{1,0:T(8,128)(2,1)S(1)} %maximum_select_fusion.27), channel_id=1, source_target_pairs={{0,2},{1,3},{2,0},{3,1},{4,6},{5,7},{6,4},{7,5},{8,10},{9,11},{10,... | collective-permute-start | bytes 2359304 | tf_op jit(solution)/shard_map/while/body/eval_jaxpr/ppermute | solution.py:20
  660.3 151.6 %reduce-scatter.11.cloned.1.call-start = ((), (), s32[]{:S(2)}) async-start(), calls=%async_computation.13 | async-start | bytes 1966080 | tf_op jit(solution)/shard_map/while/body/eval_jaxpr/reduce_scatter | solution.py:110
  703.8 37.1 %collective-permute-start.6 = (bf16[256,768]{1,0:T(8,128)(2,1)S(1)}, bf16[256,768]{1,0:T(8,128)(2,1)}, u32[]{:S(2)}, u32[]{:S(2)}) collective-permute-start(bf16[256,768]{1,0:T(8,128)(2,1)S(1)} %get-tuple-element.1648), channel_id=1, source_target_pairs={{0,1},{1,0},{2,3},{3,2},{4,5},{5,4},{6,7},{7,6},{8,9},{9,8},{10,11... | collective-permute-start | bytes 1179656 | tf_op jit(solution)/shard_map/while/body/eval_jaxpr/ppermute | solution.py:20
  743.2 16.2 %collective-permute-start.7 = (bf16[512,768]{1,0:T(8,128)(2,1)}, bf16[512,768]{1,0:T(8,128)(2,1)}, u32[]{:S(2)}, u32[]{:S(2)}) collective-permute-start(bf16[512,768]{1,0:T(8,128)(2,1)} %maximum_select_fusion.28), channel_id=1, source_target_pairs={{0,2},{1,3},{2,0},{3,1},{4,6},{5,7},{6,4},{7,5},{8,10},{9,11},{10,... | collective-permute-start | bytes 2359304 | tf_op jit(solution)/shard_map/while/body/eval_jaxpr/ppermute | solution.py:20
  814.2 103.5 %copy-start.17 = (s32[2,1024]{1,0:T(2,128)}, s32[2,1024]{1,0:T(2,128)S(1)}, u32[]{:S(2)}) copy-start(s32[2,1024]{1,0:T(2,128)S(1)} %get-tuple-element.1835) | copy-start | bytes 24580 | tf_op jit(solution)/shard_map/while
  814.2 48.4 %all-gather.21.cloned.1.call-start = ((), (), s32[]{:S(2)}) async-start(), calls=%async_computation.11 | async-start | bytes 1327104 | tf_op jit(solution)/shard_map/while/body/eval_jaxpr/all_gather | solution.py:129
  814.9 96.2 %all-gather.19.cloned.1.call-start = ((), (), s32[]{:S(2)}) async-start(), calls=%async_computation.10 | async-start | bytes 2654208 | tf_op jit(solution)/shard_map/while/body/eval_jaxpr/all_gather | solution.py:123
  815.5 141.9 %reduce-scatter.9.cloned.1.call-start = ((), (), s32[]{:S(2)}) async-start(), calls=%async_computation.12 | async-start | bytes 1966080 | tf_op jit(solution)/shard_map/while/body/eval_jaxpr/reduce_scatter | solution.py:110
  840.7 1.8 collective-permute-start.4
  842.8 19.8 %copy-start.8 = (bf16[512,768]{1,0:T(8,128)(2,1)}, bf16[512,768]{1,0:T(8,128)(2,1)S(1)}, u32[]{:S(2)}) copy-start(bf16[512,768]{1,0:T(8,128)(2,1)S(1)} %maximum_select_fusion.27) | copy-start | bytes 2359300 | tf_op jit(solution)/shard_map/while
  842.8 19.8 %collective-permute-start.5 = (bf16[512,768]{1,0:T(8,128)(2,1)S(1)}, bf16[512,768]{1,0:T(8,128)(2,1)}, u32[]{:S(2)}, u32[]{:S(2)}) collective-permute-start(bf16[512,768]{1,0:T(8,128)(2,1)S(1)} %maximum_select_fusion.27), channel_id=1, source_target_pairs={{0,2},{1,3},{2,0},{3,1},{4,6},{5,7},{6,4},{7,5},{8,10},{9,11},{10,... | collective-permute-start | bytes 2359304 | tf_op jit(solution)/shard_map/while/body/eval_jaxpr/ppermute | solution.py:20
  917.6 151.5 %reduce-scatter.11.cloned.1.call-start = ((), (), s32[]{:S(2)}) async-start(), calls=%async_computation.13 | async-start | bytes 1966080 | tf_op jit(solution)/shard_map/while/body/eval_jaxpr/reduce_scatter | solution.py:110
  961.0 36.7 %collective-permute-start.6 = (bf16[256,768]{1,0:T(8,128)(2,1)S(1)}, bf16[256,768]{1,0:T(8,128)(2,1)}, u32[]{:S(2)}, u32[]{:S(2)}) collective-permute-start(bf16[256,768]{1,0:T(8,128)(2,1)S(1)} %get-tuple-element.1648), channel_id=1, source_target_pairs={{0,1},{1,0},{2,3},{3,2},{4,5},{5,4},{6,7},{7,6},{8,9},{9,8},{10,11... | collective-permute-start | bytes 1179656 | tf_op jit(solution)/shard_map/while/body/eval_jaxpr/ppermute | solution.py:20
  1000.0 16.7 %collective-permute-start.7 = (bf16[512,768]{1,0:T(8,128)(2,1)}, bf16[512,768]{1,0:T(8,128)(2,1)}, u32[]{:S(2)}, u32[]{:S(2)}) collective-permute-start(bf16[512,768]{1,0:T(8,128)(2,1)} %maximum_select_fusion.28), channel_id=1, source_target_pairs={{0,2},{1,3},{2,0},{3,1},{4,6},{5,7},{6,4},{7,5},{8,10},{9,11},{10,... | collective-permute-start | bytes 2359304 | tf_op jit(solution)/shard_map/while/body/eval_jaxpr/ppermute | solution.py:20
  1080.3 42.6 %all-to-all-start.1 = ((bf16[8,960,96]{1,2,0:T(8,128)(2,1)}), bf16[8,960,96]{1,2,0:T(8,128)(2,1)}, u32[]{:S(2)}, u32[]{:S(2)}) async-start(bf16[8,960,96]{1,2,0:T(8,128)(2,1)} %bitcast.43), calls=%async_computation.5 | async-start | bytes 3145728 | tf_op jit(solution)/shard_map/all_to_all | solution.py:38
  1122.9 78.7 %all-to-all-start = ((bf16[8,96,2116]{2,1,0:T(8,128)(2,1)}), bf16[8,96,2116]{2,1,0:T(8,128)(2,1)S(1)}, u32[]{:S(2)}, u32[]{:S(2)}) async-start(bf16[8,96,2116]{2,1,0:T(8,128)(2,1)} %concatenate.260), calls=%async_computation.4 | async-start | bytes 6684672 | tf_op jit(solution)/shard_map/all_to_all | solution.py:38
  (119 other events, 644.9 us)
Sparse Core Ops, SparseCore 0:
  120.6 27.0 reduce-scatter.4
  149.9 52.0 all-gather.16
  204.2 39.5 all-gather.14
  250.1 26.9 reduce-scatter.6
  374.6 27.1 reduce-scatter.4
  403.9 52.0 all-gather.16
  458.2 39.5 all-gather.14
  504.1 26.9 reduce-scatter.6
  560.0 40.9 all-gather.20
  603.0 50.8 all-gather.18
  660.4 26.6 reduce-scatter.8
  784.5 27.3 reduce-scatter.10
  817.2 40.9 all-gather.20
  860.2 50.8 all-gather.18
  917.7 26.7 reduce-scatter.8
  1041.9 27.2 reduce-scatter.10
